TPU v7x, 32 devices: a whole 2x2x4 slice. The times are simulated.
32 devices in a mesh: ctx: 8 (over z, y), head: 4 (over x, core).
Axes of the slice: x: 2, y: 2, z: 4, core: 2. Of those that a mesh axis runs over, the one named last changes fastest.
Arguments:
- activations: bfloat16 [8192, 2048], P(('ctx', 'head')), may hold values from -6 to 6
- w_query: bfloat16 [2048, 1024], P('ctx', 'head'), may hold values from -0.125 to 0.125
- w_key: bfloat16 [2048, 1024], P('ctx', 'head'), may hold values from -0.125 to 0.125
- w_value: bfloat16 [2048, 2048], P('ctx', 'head'), may hold values from -0.125 to 0.125
- w_zgate: bfloat16 [2048, 2048], P('ctx', 'head'), may hold values from -0.125 to 0.125
- conv_query: bfloat16 [4, 1024], P(None, 'head'), may hold values from -3 to 3
- conv_key: bfloat16 [4, 1024], P(None, 'head'), may hold values from -3 to 3
- conv_value: bfloat16 [4, 2048], P(None, 'head'), may hold values from -3 to 3
- gate_code: int32 [8192, 16], P('ctx', 'head'), may hold values from 0 to 726816
- beta_code: int32 [8192, 16], P('ctx', 'head'), may hold values from 0 to 65536
- norm_gain: float32 [128], replicated, may hold values from 0.1 to 1.9
- w_out: bfloat16 [2048, 2048], P('head', 'ctx'), may hold values from -0.125 to 0.125
Outputs:
- layer_out: bfloat16 [8192, 2048], P(('ctx', 'head'))
All inputs are finite; a program needn't handle non-finite values.
Results may differ from a plain program's by a relative error of at most 0.012.
Values may be sent and summed in bfloat16 or wider, within the bound.
A program may use at most 192 MiB of HBM per device.

v0:
```python
import functools
import jax
import jax.numpy as jnp
from jax import lax
from jax.experimental import pallas as pl
from jax.experimental.pallas import tpu as pltpu
from jax.sharding import PartitionSpec as P

DK = 128
DV = 128
KW = 4
CHUNK = 128
EDGE = 8
SUBS = 2
NN = (((1,), (0,)), ((), ()))
NT = (((1,), (1,)), ((), ()))
TN = (((0,), (0,)), ((), ()))


def split(x):
    high = x.astype(jnp.bfloat16)
    return high, (x - high.astype(jnp.float32)).astype(jnp.bfloat16)


def dot(a, b, dims=NN):
    return lax.dot_general(a, b, dims, preferred_element_type=jnp.float32)


def dot3(a, b, dims=NN):
    return dot(a[0], b[0], dims) + (dot(a[0], b[1], dims) + dot(a[1], b[0], dims))


def dot1(a, b, dims=NN):
    return dot(a[0], b[0], dims)


INV = dot3
MAIN = dot3


def unit_inverse(lower, rows, cols):
    eye = (rows == cols).astype(jnp.float32)
    near = jnp.where((rows >> 3) == (cols >> 3), -lower, 0.0)
    first = split(near)
    second = INV(first, first)
    power = split(second)
    total = eye + near
    total = total + INV(split(total), power)
    total = total + INV(split(total), split(INV(power, power)))
    width = 3
    while (1 << width) < CHUNK:
        pair = ((rows >> (width + 1)) == (cols >> (width + 1))) & ((rows >> width) != (cols >> width))
        off = split(jnp.where(pair, lower, 0.0))
        parts = split(total)
        total = total - INV(split(INV(parts, off)), parts)
        width += 1
    return total


def delta_kernel(key_heads, group, in_ref, rim_ref, taps_ref, gate_ref, core_ref, query_ref, state_ref, rows_ref, conv_ref, run_ref):
    step = pl.program_id(0)
    heads = key_heads * group
    rows = lax.broadcasted_iota(jnp.int32, (CHUNK, CHUNK), 0)
    cols = lax.broadcasted_iota(jnp.int32, (CHUNK, CHUNK), 1)
    qw, kw, vw = key_heads * DK, key_heads * DK, heads * DV

    @pl.when(step == 0)
    def _():
        rows_ref[0:EDGE, :] = rim_ref[...].astype(jnp.float32)
        for h in range(heads):
            run_ref[h] = jnp.concatenate([(rows == cols).astype(jnp.float32), jnp.zeros((DK, DV), jnp.float32)], 1)

    @pl.when(step > 0)
    def _():
        rows_ref[0:EDGE, :] = rows_ref[CHUNK : CHUNK + EDGE, :]

    rows_ref[EDGE:, :] = in_ref[...].astype(jnp.float32)
    for c in range(0, qw + kw + vw, 128):
        acc = jnp.zeros((CHUNK, 128), jnp.float32)
        for j in range(KW):
            start = EDGE - KW + 1 + j
            acc = acc + rows_ref[start : start + CHUNK, c : c + 128] * taps_ref[j : j + 1, c : c + 128].astype(jnp.float32)
        conv_ref[:, c : c + 128] = jax.nn.silu(acc).astype(jnp.bfloat16)

    gates = gate_ref[...]
    tri = (rows >= cols).astype(jnp.bfloat16)
    g1 = gates.astype(jnp.bfloat16)
    rest = gates - g1.astype(jnp.float32)
    g2 = rest.astype(jnp.bfloat16)
    g3 = (rest - g2.astype(jnp.float32)).astype(jnp.bfloat16)
    cum = dot(tri, g1) + (dot(tri, g2) + dot(tri, g3))
    cum_t = jnp.transpose(cum)
    strict = rows > cols
    incl = rows >= cols
    for kh in range(key_heads):
        q = conv_ref[:, kh * DK : (kh + 1) * DK]
        k_raw = conv_ref[:, qw + kh * DK : qw + (kh + 1) * DK].astype(jnp.float32)
        khat = k_raw / jnp.sqrt(jnp.sum(k_raw * k_raw, -1, keepdims=True) + 1e-06)
        ks = split(khat)
        gram = MAIN(ks, ks, NT)
        qk = dot(q, ks[0], NT) + dot(q, ks[1], NT)
        for r in range(group):
            h = kh * group + r
            col = cum[:, h : h + 1]
            row = cum_t[h : h + 1, :]
            beta = gates[:, heads + h : heads + h + 1]
            last = cum[CHUNK - 1 : CHUNK, h : h + 1]
            decay = jnp.exp(jnp.minimum(col - row, 0.0))
            lower = jnp.where(strict, beta * gram * decay, 0.0)
            inverse = split(unit_inverse(lower, rows, cols))
            grown = jnp.exp(col)
            v = conv_ref[:, qw + kw + h * DV : qw + kw + (h + 1) * DV].astype(jnp.float32)
            right = split(jnp.concatenate([khat * (beta * grown), v * beta], 1))
            wu = MAIN(inverse, right)
            scores = split(jnp.where(incl, qk * decay, 0.0))
            tail = split(khat * jnp.exp(last - col))
            run = run_ref[h]
            runs = split(run)
            y = jnp.concatenate([jnp.zeros((CHUNK, DK), jnp.float32), wu[:, DK:]], 1) - MAIN(split(wu[:, :DK]), runs)
            ys = split(y)
            out = grown * (dot(q, runs[0]) + dot(q, runs[1])) + MAIN(scores, ys)
            run_ref[h] = jnp.exp(last) * run + MAIN(tail, ys, TN)
            query_ref[:, h * DK : (h + 1) * DK] = out[:, :DK]
            core_ref[:, h * DV : (h + 1) * DV] = out[:, DK:]

    @pl.when(step == pl.num_programs(0) - 1)
    def _():
        state_ref[...] = run_ref[...].astype(state_ref.dtype)


def delta(joined, rim, taps, gates, key_width, heads):
    length = joined.shape[0]
    key_heads = key_width // DK
    width = rim.shape[1]
    step_rows = lambda n: pl.BlockSpec((CHUNK, n), lambda i: (i, 0))
    whole = lambda *shape: pl.BlockSpec(shape, lambda i: (0,) * len(shape))
    return pl.pallas_call(
        functools.partial(delta_kernel, key_heads, heads // key_heads),
        grid=(length // CHUNK,),
        in_specs=[step_rows(width), whole(EDGE, width), whole(KW, width), step_rows(gates.shape[1])],
        out_specs=[step_rows(heads * DV), step_rows(heads * DK), whole(heads, DK, DK + DV)],
        out_shape=[
            jax.ShapeDtypeStruct((length, heads * DV), jnp.float32),
            jax.ShapeDtypeStruct((length, heads * DK), jnp.float32),
            jax.ShapeDtypeStruct((heads, DK, DK + DV), jnp.bfloat16),
        ],
        scratch_shapes=[
            pltpu.VMEM((CHUNK + EDGE, width), jnp.float32),
            pltpu.VMEM((CHUNK, width), jnp.bfloat16),
            pltpu.VMEM((heads, DK, DK + DV), jnp.float32),
        ],
        cost_estimate=pl.CostEstimate(flops=60 * 10**9, bytes_accessed=8 * 10**6, transcendentals=10**6),
        name="delta",
    )(joined, rim, taps, gates)


def finish_kernel(count, heads, core_ref, query_ref, z_ref, maps_ref, gain_ref, out_ref, state_ref):
    mine = lax.axis_index("ctx")

    @pl.when(pl.program_id(0) == 0)
    def _():
        state_ref[...] = jnp.zeros_like(state_ref)

        def hop(p, carry):
            @pl.when(p < mine)
            def _():
                for h in range(heads):
                    s = split(state_ref[h])
                    trans = maps_ref[p, h, :, :DK]
                    state_ref[h] = dot(trans, s[0]) + dot(trans, s[1]) + maps_ref[p, h, :, DK:].astype(jnp.float32)

            return carry

        lax.fori_loop(0, count - 1, hop, 0)

    for h in range(heads):
        span = slice(h * DV, (h + 1) * DV)
        core = core_ref[:, span] + MAIN(split(query_ref[:, span]), split(state_ref[h]))
        z = z_ref[:, span].astype(jnp.float32)
        mean = jnp.mean(core * core, -1, keepdims=True)
        out_ref[:, span] = (core * lax.rsqrt(mean + 1e-06) * gain_ref[...] * jax.nn.silu(z)).astype(jnp.bfloat16)


def finish(core, query, joined, maps, gain):
    length, wide = core.shape
    count, heads = maps.shape[:2]
    tile = min(256, length)
    step_rows = pl.BlockSpec((tile, wide), lambda i: (i, 0))
    return pl.pallas_call(
        functools.partial(finish_kernel, count, heads),
        grid=(length // tile,),
        in_specs=[step_rows, step_rows, pl.BlockSpec((tile, wide), lambda i: (i, joined.shape[1] // wide - 1)), pl.BlockSpec(maps.shape, lambda i: (0, 0, 0, 0)), pl.BlockSpec((1, DV), lambda i: (0, 0))],
        out_specs=step_rows,
        out_shape=jax.ShapeDtypeStruct((length, wide), jnp.bfloat16),
        scratch_shapes=[pltpu.VMEM((heads, DK, DV), jnp.float32)],
        cost_estimate=pl.CostEstimate(flops=10**9, bytes_accessed=8 * 10**6, transcendentals=10**6),
        name="finish",
    )(core, query, joined, maps, gain)


def ring_device(position, n):
    odd = lax.div(position, n // 2)
    return (1 - odd) * (2 * position) + odd * (2 * (n - 1 - position) + 1)


def gather_kernel(n, heads, act_ref, w_ref, act_out, w_out, act_tmp, w_tmp, local_sem, act_send, act_recv, ring_send, ring_recv):
    ctx, head = lax.axis_index("ctx"), lax.axis_index("head")
    odd = lax.rem(ctx, 2)
    position = (1 - odd) * lax.div(ctx, 2) + odd * (n - 1 - lax.div(ctx, 2))
    after = ring_device(lax.rem(position + 1, n), n)
    before = ring_device(lax.rem(position + n - 1, n), n)
    peers = [lax.rem(head + d, heads) for d in range(1, heads)]

    barrier = pltpu.get_barrier_semaphore()
    for other in (after, before):
        pl.semaphore_signal(barrier, inc=1, device_id=(other, head), device_id_type=pl.DeviceIdType.MESH)
    for peer in peers:
        pl.semaphore_signal(barrier, inc=1, device_id=(ctx, peer), device_id_type=pl.DeviceIdType.MESH)
    pl.semaphore_wait(barrier, heads + 1)

    piece = w_ref.shape[0] // (2 * SUBS)

    def hop(s, way, sub):
        offset = (way * SUBS + sub) * piece
        owner = ring_device(lax.rem(position + (n - s if way == 0 else s), n), n)
        place = w_out.at[owner, pl.ds(offset, piece)]
        return pltpu.make_async_remote_copy(
            src_ref=w_ref.at[pl.ds(offset, piece)] if s == 0 else place,
            dst_ref=place,
            send_sem=ring_send.at[s, way * SUBS + sub],
            recv_sem=ring_recv.at[s, way * SUBS + sub],
            device_id=(after if way == 0 else before, head),
            device_id_type=pl.DeviceIdType.MESH,
        )

    hops = [[hop(s, way, sub) for sub in range(SUBS) for way in range(2)] for s in range(n - 1)]
    for copy in hops[0]:
        copy.start()
    sends = [
        pltpu.make_async_remote_copy(
            src_ref=act_ref,
            dst_ref=act_out.at[head],
            send_sem=act_send.at[d],
            recv_sem=act_recv.at[d],
            device_id=(ctx, peer),
            device_id_type=pl.DeviceIdType.MESH,
        )
        for d, peer in enumerate(peers)
    ]
    for copy in sends:
        copy.start()
    take = [pltpu.make_async_copy(act_ref, act_tmp, local_sem.at[0]), pltpu.make_async_copy(w_ref, w_tmp, local_sem.at[1])]
    keep = [
        pltpu.make_async_copy(act_tmp, act_out.at[head], local_sem.at[2]),
        pltpu.make_async_copy(w_tmp, w_out.at[ctx], local_sem.at[3]),
    ]
    for copy in take:
        copy.start()
    for one, two in zip(take, keep):
        one.wait()
        two.start()
    for s in range(1, n - 1):
        for arrived, copy in zip(hops[s - 1], hops[s]):
            arrived.wait_recv()
            copy.start()
    for copy in hops[n - 2]:
        copy.wait_recv()
    for copy in sends:
        copy.wait_recv()
    for two in keep:
        two.wait()
    for copy in sends:
        copy.wait_send()
    for row in hops:
        for copy in row:
            copy.wait_send()


def gather_inputs(activations, weights):
    n, heads = lax.axis_size("ctx"), lax.axis_size("head")
    anywhere = pl.BlockSpec(memory_space=pl.ANY)
    act, w = pl.pallas_call(
        functools.partial(gather_kernel, n, heads),
        in_specs=[anywhere, anywhere],
        out_specs=[anywhere, anywhere],
        out_shape=[
            jax.ShapeDtypeStruct((heads,) + activations.shape, activations.dtype),
            jax.ShapeDtypeStruct((n,) + weights.shape, weights.dtype),
        ],
        scratch_shapes=[
            pltpu.VMEM(activations.shape, activations.dtype),
            pltpu.VMEM(weights.shape, weights.dtype),
            pltpu.SemaphoreType.DMA((4,)),
            pltpu.SemaphoreType.DMA((heads - 1,)),
            pltpu.SemaphoreType.DMA((heads - 1,)),
            pltpu.SemaphoreType.DMA((n - 1, 2 * SUBS)),
            pltpu.SemaphoreType.DMA((n - 1, 2 * SUBS)),
        ],
        compiler_params=pltpu.CompilerParams(collective_id=0, has_side_effects=True),
        name="gather_inputs",
    )(activations, weights)
    return act.reshape(-1, act.shape[-1]), w.reshape(-1, w.shape[-1])


def shards(activations, w_query, w_key, w_value, w_zgate, conv_query, conv_key, conv_value, gate_code, beta_code, norm_gain, w_out):
    count = lax.axis_size("ctx")
    gathered, weight = gather_inputs(activations, jnp.concatenate([w_query, w_key, w_value, w_zgate], 1))
    length = gathered.shape[0]
    conv_width = conv_query.shape[1] + conv_key.shape[1] + conv_value.shape[1]
    project = lambda x, w: jnp.dot(x, w, preferred_element_type=jnp.float32).astype(jnp.bfloat16)
    edge = lax.ppermute(gathered[length - EDGE :], "ctx", [(i, i + 1) for i in range(count - 1)])
    rim = project(edge, weight[:, :conv_width])
    joined = project(gathered, weight)
    heads = gate_code.shape[1]
    gates = jnp.concatenate(
        [
            -gate_code.astype(jnp.float32) / 1048576.0,
            beta_code.astype(jnp.float32) / 65536.0,
            jnp.zeros((length, 128 - 2 * heads), jnp.float32),
        ],
        1,
    )
    taps = jnp.concatenate([conv_query, conv_key, conv_value], 1)
    w_out, joined = lax.optimization_barrier((w_out, joined))
    out_weight = lax.all_gather(w_out, "ctx", axis=1, tiled=True)
    core, query, state = delta(joined, rim, taps, gates, conv_query.shape[1], heads)
    maps = lax.all_gather(state, "ctx", axis=0)
    normed = finish(core, query, joined, maps, norm_gain.reshape(1, DV))
    mixed = jnp.dot(normed, out_weight, preferred_element_type=jnp.float32).astype(jnp.bfloat16)
    return lax.psum_scatter(mixed, "head", scatter_dimension=0, tiled=True)


def solution(mesh):
    return jax.shard_map(
        shards,
        mesh=mesh,
        in_specs=(
            P(("ctx", "head"), None),
            P("ctx", "head"),
            P("ctx", "head"),
            P("ctx", "head"),
            P("ctx", "head"),
            P(None, "head"),
            P(None, "head"),
            P(None, "head"),
            P("ctx", "head"),
            P("ctx", "head"),
            P(),
            P("head", "ctx"),
        ),
        out_specs=P(("ctx", "head"), None),
        check_vma=False,
    )
```

profile of v0, /device:TPU:0, one launch (start us, length us, event | category | flops | bytes accessed | tf_op | source)
XLA Modules:
  0.0 333.1 jit_solution(1932013318473110390)
XLA Ops:
  6.5 0.0 all-gather.6.cloned.1.call-start
  6.5 2.0 pad_maximum_fusion.w_ref
  8.6 65.5 %gather_inputs.1 = (bf16[4,256,2048]{2,1,0:T(8,128)(2,1)}, bf16[8,256,1536]{2,1,0:T(8,128)(2,1)}) custom-call(bf16[256,2048]{1,0:T(8,128)(2,1)} %act_ref.1, bf16[256,1536]{1,0:T(8,128)(2,1)} %pad_maximum_fusion.w_ref), custom_call_target="tpu_custom_call" | custom-call | tf_op jit(solution)/shard_map/gather_inputs/pallas_call | solution.py:282
  74.0 0.8 slice.8
  74.8 3.4 %collective-permute-start = (bf16[8,2048]{1,0:T(8,128)(2,1)S(1)}, bf16[8,2048]{1,0:T(8,128)(2,1)S(1)}, u32[]{:S(2)}, u32[]{:S(2)}) collective-permute-start(bf16[8,2048]{1,0:T(8,128)(2,1)S(1)} %slice.8), channel_id=1, source_target_pairs={{0,4},{4,8},{8,12},{12,16},{16,20},{20,24},{24,28},{1,5},{5,9},{9,... | collective-permute-start | bytes 98312 | tf_op jit(solution)/shard_map/ppermute | solution.py:311
  78.2 0.0 copy-start
  78.2 0.0 copy-start.1
  78.2 0.0 copy-start.2
  78.3 0.0 copy-start.3
  78.3 0.0 copy-start.4
  78.3 11.2 %convolution_convert_fusion.in_ref.z_ref = bf16[1024,1536]{1,0:T(8,128)(2,1)} fusion(bf16[1024,2048]{1,0:T(8,128)(2,1)} %bitcast.14, bf16[2048,1536]{1,0:T(8,128)(2,1)} %bitcast.9), kind=kOutput, calls=%fused_computation.2 | convolution fusion | flops 6444023808 | bytes 13631488 | tf_op jit(solution)/shard_map/dot_general | solution.py:310
  89.5 0.0 copy-done
  89.5 0.2 copy.20
  89.7 0.0 copy-done.1
  89.8 0.2 copy.21
  90.0 0.1 pad.2.clone
  90.1 1.0 maximum_maximum_fusion.gate_ref
  91.1 0.0 copy-done.2
  91.1 0.6 pad_maximum_fusion.1.taps_ref
  91.7 0.0 collective-permute-done
  91.7 3.4 %fusion.2.rim_ref = bf16[8,1024]{1,0:T(8,128)(2,1)} fusion(bf16[8,2048]{1,0:T(8,128)(2,1)S(1)} %collective-permute-done, bf16[2048,1536]{1,0:T(8,128)(2,1)} %bitcast.10), kind=kOutput, calls=%fused_computation.4 | convolution fusion | flops 33562624 | bytes 4243456 | tf_op jit(solution)/shard_map/dot_general | solution.py:310
  95.1 82.8 %delta.1 = (f32[1024,512]{1,0:T(8,128)}, f32[1024,512]{1,0:T(8,128)}, bf16[4,128,256]{2,1,0:T(8,128)(2,1)}) custom-call(bf16[1024,1536]{1,0:T(8,128)(2,1)} %convolution_convert_fusion.in_ref.z_ref, bf16[8,1024]{1,0:T(8,128)(2,1)} %fusion.2.rim_ref, bf16[4,1024]{1,0:T(4,128)(2,1)} %pad_maximum_fusion.1.taps_ref, f32[1024,128]{1,0:T(8,128)} %maximum_maximum_fusion.gate_ref), custom_call_target="tpu_custom_call" | custom-call | flops 60000002048 | bytes 8000000 | tf_op jit(solution)/shard_map/delta/pallas_call | solution.py:137
  178.0 0.0 all-gather.6.cloned.1.call-update
  178.0 0.0 all-gather.4.cloned.1.call-start
  178.0 0.7 all-gather.4.cloned.1.call-update
  178.7 0.0 reduce-scatter.2.cloned.1.call-start
  178.8 47.7 %all-gather.6.cloned.1.call-done = bf16[32,128,256]{2,1,0:T(8,128)(2,1)} async-done(((bf16[4,128,256]{2,1,0:T(8,128)(2,1)}), bf16[32,128,256]{2,1,0:T(8,128)(2,1)}) %all-gather.6.cloned.1.call-update) | async-done | bytes 2097168 | tf_op jit(solution)/shard_map/all_gather | solution.py:327
  226.5 6.0 %finish.1 = bf16[1024,512]{1,0:T(8,128)(2,1)} custom-call(f32[1024,512]{1,0:T(8,128)} %get-tuple-element.15.core_ref, f32[1024,512]{1,0:T(8,128)} %get-tuple-element.16.query_ref, bf16[1024,1536]{1,0:T(8,128)(2,1)} %convolution_convert_fusion.in_ref.z_ref, bf16[8,4,128,256]{3,2,1,0:T(8,128)(2,1)} %bitcast.11, f32[1,128]{1,0:T(1,128)} %bitcast.12), custom_call_target="tpu_custom_call" | custom-call | flops 1000000000 | bytes 8000000 | tf_op jit(solution)/shard_map/finish/pallas_call | solution.py:189
  232.5 44.9 %all-gather.4.cloned.1.call-done = bf16[512,2048]{1,0:T(8,128)(2,1)} async-done(((bf16[512,256]{1,0:T(8,128)(2,1)}), bf16[512,2048]{1,0:T(8,128)(2,1)}) %all-gather.4.cloned.1.call-update) | async-done | bytes 2097168 | tf_op jit(solution)/shard_map/all_gather | solution.py:325
  277.4 6.2 %convolution_convert_fusion.1 = bf16[1024,2048]{1,0:T(8,128)(2,1)} fusion(bf16[1024,512]{1,0:T(8,128)(2,1)} %finish.1, bf16[512,2048]{1,0:T(8,128)(2,1)} %all-gather.4.cloned.1.call-done), kind=kOutput, calls=%fused_computation.3 | convolution fusion | flops 2149580800 | bytes 7340032 | tf_op jit(solution)/shard_map/dot_general | solution.py:329
  283.6 0.0 reduce-scatter.2.cloned.1.call-update
  283.7 42.9 %reduce-scatter.2.cloned.1.call-done = bf16[256,2048]{1,0:T(8,128)(2,1)} async-done(((bf16[1024,2048]{1,0:T(8,128)(2,1)}), bf16[256,2048]{1,0:T(8,128)(2,1)}) %reduce-scatter.2.cloned.1.call-update) | async-done | bytes 1048592 | tf_op jit(solution)/shard_map/reduce_scatter | solution.py:330
  (5 shorter events, 0.0 us)
Async XLA Ops:
  6.5 219.9 %all-gather.6.cloned.1.call-start = ((), (), s32[]{:S(2)}) async-start(), calls=%async_computation.3 | async-start | bytes 2359296 | tf_op jit(solution)/shard_map/all_gather | solution.py:327
  74.8 16.9 %collective-permute-start = (bf16[8,2048]{1,0:T(8,128)(2,1)S(1)}, bf16[8,2048]{1,0:T(8,128)(2,1)S(1)}, u32[]{:S(2)}, u32[]{:S(2)}) collective-permute-start(bf16[8,2048]{1,0:T(8,128)(2,1)S(1)} %slice.8), channel_id=1, source_target_pairs={{0,4},{4,8},{8,12},{12,16},{16,20},{20,24},{24,28},{1,5},{5,9},{9,... | collective-permute-start | bytes 98312 | tf_op jit(solution)/shard_map/ppermute | solution.py:311
  78.2 11.3 %copy-start = (s32[1024,4]{0,1:T(4,128)S(1)}, s32[1024,4]{0,1:T(4,128)}, u32[]{:S(2)}) copy-start(s32[1024,4]{0,1:T(4,128)} %param.20) | copy-start | bytes 49156
  78.2 11.5 %copy-start.1 = (s32[1024,4]{0,1:T(4,128)S(1)}, s32[1024,4]{0,1:T(4,128)}, u32[]{:S(2)}) copy-start(s32[1024,4]{0,1:T(4,128)} %param.21) | copy-start | bytes 49156
  78.2 12.8 %copy-start.2 = (bf16[4,512]{1,0:T(4,128)(2,1)S(1)}, bf16[4,512]{1,0:T(4,128)(2,1)}, u32[]{:S(2)}) copy-start(bf16[4,512]{1,0:T(4,128)(2,1)} %param.19) | copy-start | bytes 12292
  78.3 12.8 %copy-start.3 = (bf16[4,256]{1,0:T(4,128)(2,1)S(1)}, bf16[4,256]{1,0:T(4,128)(2,1)}, u32[]{:S(2)}) copy-start(bf16[4,256]{1,0:T(4,128)(2,1)} %param.18) | copy-start | bytes 6148
  78.3 12.8 %copy-start.4 = (bf16[4,256]{1,0:T(4,128)(2,1)S(1)}, bf16[4,256]{1,0:T(4,128)(2,1)}, u32[]{:S(2)}) copy-start(bf16[4,256]{1,0:T(4,128)(2,1)} %param.17) | copy-start | bytes 6148
  178.0 99.4 %all-gather.4.cloned.1.call-start = ((), (), s32[]{:S(2)}) async-start(), calls=%async_computation.1 | async-start | bytes 2359296 | tf_op jit(solution)/shard_map/all_gather | solution.py:325
  178.7 147.8 %reduce-scatter.2.cloned.1.call-start = ((), (), s32[]{:S(2)}) async-start(), calls=%async_computation.2 | async-start | bytes 5242880 | tf_op jit(solution)/shard_map/reduce_scatter | solution.py:330
Sparse Core Ops, SparseCore 0:
  178.1 48.3 all-gather.5
  228.5 48.8 all-gather.3
  283.8 42.7 reduce-scatter.1
where the time goes:
time: 333 us
  Pallas kernels  154 us (46%)
  waiting for transfers between devices  136 us (41%)
  matrix products  20.9 us (6%)
  between operations  13.2 us (4%)
  other arithmetic  3.64 us (1%)
  starting transfers between devices  3.5 us (1%)
    pallas_call x1, Pallas kernels, delta(): pl.pallas_call(functools.partial(delta_kernel, key_heads, heads // key_he...  82.8 us
    pallas_call x1, Pallas kernels, gather_inputs(): pl.pallas_call(functools.partial(gather_kernel, n, heads), in_specs=[anyw...  65.5 us
    all_gather x1, waiting for transfers between devices, shards(): maps = lax.all_gather(state, 'ctx', axis=0)  47.7 us
    all_gather x1, waiting for transfers between devices, shards(): out_weight = lax.all_gather(w_out, 'ctx', axis=1, tiled=True)  44.9 us
    reduce_scatter x1, waiting for transfers between devices, shards(): return lax.psum_scatter(mixed, 'head', scatter_dimension=0, tiled=True)  42.9 us
    dot_general x2, matrix products, shards(): jnp.dot(x, w, preferred_element_type=jnp.float32).astype(jnp.bfloat16)  14.7 us
  transfers between devices with their start and end apart: 4, of which 3 were waited for; matrix products, arithmetic and copies ran while one was open for 4% of the time, Pallas kernels for 2%

commit v1 on v0

v1 whole, which is shorter than its diff:
```python
import functools
import jax
import jax.numpy as jnp
from jax import lax
from jax.experimental import pallas as pl
from jax.experimental.pallas import tpu as pltpu
from jax.sharding import PartitionSpec as P

DK = 128
DV = 128
KW = 4
CHUNK = 128
RIM = 16
PAIR = 2
MESH = pl.DeviceIdType.MESH
NN = (((1,), (0,)), ((), ()))
NT = (((1,), (1,)), ((), ()))
BF = jnp.bfloat16
F32 = jnp.float32


def dot(a, b, dims=NN):
    return lax.dot_general(a, b, dims, preferred_element_type=F32)


def silu(x):
    half = 0.5 * x
    return half + half * jnp.tanh(half)


def ring_device(position, n):
    odd = lax.div(position, n // 2)
    return (1 - odd) * (2 * position) + odd * (2 * (n - 1 - position) + 1)


class Stream:
    def __init__(self, n, view, send, recv):
        ctx, head = lax.axis_index("ctx"), lax.axis_index("head")
        odd = lax.rem(ctx, 2)
        position = (1 - odd) * lax.div(ctx, 2) + odd * (n - 1 - lax.div(ctx, 2))
        after = ring_device(lax.rem(position + 1, n), n)
        before = ring_device(lax.rem(position + n - 1, n), n)
        self.reach = n // 2
        self.units = {}
        for s in range(self.reach):
            for way in range(2):
                for half in range(2):
                    if s == self.reach - 1 and half != way:
                        continue
                    owner = ring_device(lax.rem(position + (n - s if way == 0 else s), n), n)
                    index = (s * 2 + way) * 2 + half
                    place = view(owner, half)
                    self.units[s, way, half] = pltpu.make_async_remote_copy(
                        src_ref=place,
                        dst_ref=place,
                        send_sem=send.at[index],
                        recv_sem=recv.at[index],
                        device_id=(after if way == 0 else before, head),
                        device_id_type=MESH,
                    )
        self.owner = lambda s, way: ring_device(lax.rem(position + (n - s if way == 0 else s), n), n)
        self.waited = set()

    def start(self):
        for half in range(2):
            for way in range(2):
                if (0, way, half) in self.units:
                    self.units[0, way, half].start()

    def relay(self, s):
        for half in range(2):
            for way in range(2):
                if (s, way, half) in self.units:
                    self.units[s - 1, way, half].wait_recv()
                    self.waited.add((s - 1, way, half))
                    self.units[s, way, half].start()

    def finish(self):
        for key, unit in self.units.items():
            if key not in self.waited:
                unit.wait_recv()

    def drain(self):
        for unit in self.units.values():
            unit.wait_send()


def unit_inverse(lowers, rows, cols):
    eye = (rows == cols).astype(F32)
    same = (rows >> 3) == (cols >> 3)
    nears = [jnp.where(same, -x, 0.0) for x in lowers]
    firsts = [x.astype(BF) for x in nears]
    powers = [dot(x, x).astype(BF) for x in firsts]
    totals = [eye + x for x in nears]
    totals = [t + dot(t.astype(BF), p) for t, p in zip(totals, powers)]
    powers = [dot(p, p).astype(BF) for p in powers]
    totals = [t + dot(t.astype(BF), p) for t, p in zip(totals, powers)]
    width = 3
    while (1 << width) < CHUNK:
        pair = ((rows >> (width + 1)) == (cols >> (width + 1))) & ((rows >> width) != (cols >> width))
        parts = [t.astype(BF) for t in totals]
        offs = [jnp.where(pair, x, 0.0).astype(BF) for x in lowers]
        mids = [dot(t, o).astype(BF) for t, o in zip(parts, offs)]
        totals = [t - dot(m, p) for t, m, p in zip(totals, mids, parts)]
        width += 1
    return totals


def layer_kernel(
    n, heads, key_heads, group, wide,
    act_ref, wq_ref, wk_ref, wv_ref, wz_ref, wo_ref, cq_ref, ck_ref, cv_ref, gate_ref, beta_ref, gain_ref,
    out_ref,
    act, weight, mix, raw, zed, gates, wu, lhs, rhs, tails, run, core, query, maps, norm, norm_all,
    local_sem, act_send, act_recv, rim_send, rim_recv, ring_send, ring_recv, map_send, map_recv, mix_send, mix_recv, norm_send, norm_recv,
):
    ctx, head = lax.axis_index("ctx"), lax.axis_index("head")
    one = head + 1 - 2 * lax.rem(head, 2)
    two = lax.rem(head + 2, heads)
    three = lax.rem(one + 2, heads)
    rows = act_ref.shape[0]
    length = rows * heads
    depth = wq_ref.shape[0]
    chunks = length // CHUNK
    span = 2 * DK + group * DV

    def weight_view(g):
        def view(owner, half):
            return weight.at[g, pl.ds(pl.multiple_of(owner * depth + half * (depth // 2), depth // 2), depth // 2)]

        return view

    def mix_slot(h, owner, half=None):
        size = mix.shape[2] if wide else wo_ref.shape[0]
        if wide:
            return mix.at[h, owner] if half is None else mix.at[h, owner, pl.ds(half * (size // 2), size // 2)]
        if half is None:
            return mix.at[h, pl.ds(pl.multiple_of(owner * size, size), size)]
        return mix.at[h, pl.ds(pl.multiple_of(owner * size + half * (size // 2), size // 2), size // 2)]

    place = pl.ds(pl.multiple_of(ctx * depth, depth), depth)
    mine = []
    for g in range(key_heads):
        mine.append((wq_ref.at[:, pl.ds(g * DK, DK)], weight.at[g, place, pl.ds(0, DK)]))
        mine.append((wk_ref.at[:, pl.ds(g * DK, DK)], weight.at[g, place, pl.ds(DK, DK)]))
        mine.append((wv_ref.at[:, pl.ds(g * group * DV, group * DV)], weight.at[g, place, pl.ds(2 * DK, group * DV)]))
    mine.append((wz_ref, weight.at[key_heads, place]))
    mine.append((wo_ref, mix_slot(head, ctx)))
    block = lambda h, sub: act.at[pl.ds(pl.multiple_of(RIM + h * rows + sub * (rows // PAIR), 16), rows // PAIR)]
    piece = lambda sub: act_ref.at[pl.ds(sub * (rows // PAIR), rows // PAIR)]
    for sub in range(PAIR):
        mine.append((piece(sub), block(head, sub)))
    mine = [pltpu.make_async_copy(a, b, local_sem.at[i]) for i, (a, b) in enumerate(mine)]
    for copy in mine:
        copy.start()

    barrier = pltpu.get_barrier_semaphore()
    odd = lax.rem(ctx, 2)
    position = (1 - odd) * lax.div(ctx, 2) + odd * (n - 1 - lax.div(ctx, 2))
    for step in (1, n - 1):
        other = ring_device(lax.rem(position + step, n), n)
        pl.semaphore_signal(barrier, inc=1, device_id=(other, head), device_id_type=MESH)
    for peer in (one, two, three):
        pl.semaphore_signal(barrier, inc=1, device_id=(ctx, peer), device_id_type=MESH)
    gives_rim = (head == heads - 1) & (ctx < n - 1)

    @pl.when(ctx > 0)
    def _():
        pl.semaphore_signal(barrier, inc=1, device_id=(ctx - 1, heads - 1), device_id_type=MESH)

    pl.semaphore_wait(barrier, 5 + heads * gives_rim.astype(jnp.int32))

    def to_peer(src, dst, index, peer):
        return pltpu.make_async_remote_copy(
            src_ref=src, dst_ref=dst, send_sem=act_send.at[index], recv_sem=act_recv.at[index], device_id=(ctx, peer), device_id_type=MESH
        )

    across = [to_peer(piece(s), block(head, s), s, two) for s in range(PAIR)]
    beside = [to_peer(piece(s), block(head, s), PAIR + s, one) for s in range(PAIR)]
    onward = [to_peer(block(two, s), block(two, s), 2 * PAIR + s, one) for s in range(PAIR)]
    rims = [
        pltpu.make_async_remote_copy(
            src_ref=act_ref.at[pl.ds(rows - RIM, RIM)],
            dst_ref=act.at[pl.ds(0, RIM)],
            send_sem=rim_send.at[h],
            recv_sem=rim_recv,
            device_id=(lax.rem(ctx + 1, n), h),
            device_id_type=MESH,
        )
        for h in range(heads)
    ]
    streams = [Stream(n, weight_view(g), ring_send.at[g], ring_recv.at[g]) for g in range(key_heads + 1)]
    mixes = Stream(n, lambda owner, half: mix_slot(head, owner, half), ring_send.at[key_heads + 1], ring_recv.at[key_heads + 1])
    map_streams = [
        Stream(n, lambda owner, half, g=g: maps.at[g, owner, pl.ds(half * group * DK // 2, group * DK // 2)], map_send.at[g], map_recv.at[g])
        for g in range(key_heads)
    ]

    @pl.when(gives_rim)
    def _():
        for copy in rims:
            copy.start()

    for copy in across:
        copy.start()
    for copy in beside:
        copy.start()
    for copy in mine:
        copy.wait()

    @pl.when(ctx == 0)
    def _():
        act[0:RIM, :] = jnp.zeros((RIM, act.shape[1]), BF)

    streams[0].start()

    iota = lambda dim: lax.broadcasted_iota(jnp.int32, (CHUNK, CHUNK), dim)
    tri = (iota(0) <= iota(1)).astype(BF)
    decays = gate_ref[...].astype(F32) * (-1.0 / 1048576.0)
    betas = beta_ref[...].astype(F32) * (1.0 / 65536.0)
    values = key_heads * group
    stacked = jnp.concatenate([decays[:, c * CHUNK : (c + 1) * CHUNK] for c in range(chunks)], 0)
    g1 = stacked.astype(BF)
    rest = stacked - g1.astype(F32)
    g2 = rest.astype(BF)
    g3 = (rest - g2.astype(F32)).astype(BF)
    sums = dot(g1, tri) + (dot(g2, tri) + dot(g3, tri))
    for g in range(key_heads):
        for c in range(chunks):
            for r in range(group):
                h = g * group + r
                gates[g, c, r : r + 1, :] = sums[c * values + h : c * values + h + 1, :]
                gates[g, c, group + r : group + r + 1, :] = betas[h : h + 1, c * CHUNK : (c + 1) * CHUNK]
            gates[g, c, 2 * group :, :] = jnp.zeros((8 - 2 * group, CHUNK), F32)

    def relay_all(stream):
        for s in range(1, stream.reach):
            stream.relay(s)

    for s in range(1, streams[0].reach):
        streams[0].relay(s)
    for stream in streams[1:]:
        stream.start()
        relay_all(stream)
    mixes.start()
    relay_all(mixes)
    for a, b in zip(across, onward):
        a.wait_recv()
        b.start()

    @pl.when(ctx > 0)
    def _():
        rims[0].wait_recv()

    for copy in beside + onward:
        copy.wait_recv()
    for stream in streams + [mixes]:
        stream.finish()

    def mix_copy(src, index, peer):
        return pltpu.make_async_remote_copy(
            src_ref=src, dst_ref=src, send_sem=mix_send.at[index], recv_sem=mix_recv.at[index], device_id=(ctx, peer), device_id_type=MESH
        )

    mix_across = mix_copy(mix.at[head], 0, two)
    mix_beside = mix_copy(mix.at[head], 1, one)
    mix_onward = mix_copy(mix.at[two], 2, one)
    mix_across.start()
    mix_beside.start()

    def project(g, store):
        tile = (length + RIM) // 5

        def body(m, carry):
            start = pl.multiple_of(m * tile, 16)
            store(start, tile, dot(act[pl.ds(start, tile), :], weight[g]))
            return carry

        lax.fori_loop(0, 5, body, 0)

    def store_raw(start, tile, value):
        raw[pl.ds(start, tile), :] = value

    def store_zed(start, tile, value):
        zed[pl.ds(start, tile), :] = silu(value)

    def within(g, chunk_list):
        row_id, col_id = iota(0), iota(1)
        strict, incl = row_id > col_id, row_id >= col_id
        taps = [
            jnp.concatenate(
                [
                    cq_ref[j : j + 1, g * DK : (g + 1) * DK],
                    ck_ref[j : j + 1, g * DK : (g + 1) * DK],
                    cv_ref[j : j + 1, g * group * DV : (g + 1) * group * DV],
                ],
                1,
            ).astype(F32)
            for j in range(KW)
        ]
        items, lowers = [], []
        for c in chunk_list:
            x = raw[pl.ds(pl.multiple_of(c * CHUNK, CHUNK), CHUNK + RIM), :]
            acc = x[RIM - KW + 1 : RIM - KW + 1 + CHUNK] * taps[0]
            for j in range(1, KW):
                acc = acc + x[RIM - KW + 1 + j : RIM - KW + 1 + j + CHUNK] * taps[j]
            conv = silu(acc)
            q, k = conv[:, :DK], conv[:, DK : 2 * DK]
            khat = k * lax.rsqrt(jnp.sum(k * k, -1, keepdims=True) + 1e-06)
            turned = jnp.transpose(khat)
            both = jnp.concatenate([q.astype(BF), khat.astype(BF)], 0)
            pairs = dot(both, turned.astype(BF))
            qk, gram = pairs[:CHUNK], pairs[CHUNK:]
            info = gates[g, c]
            info_t = jnp.transpose(info)
            for r in range(group):
                row, col = info[r : r + 1, :], info_t[:, r : r + 1]
                beta = info_t[:, group + r : group + r + 1]
                decay = jnp.exp(jnp.minimum(col - row, 0.0))
                lowers.append(jnp.where(strict, beta * gram * decay, 0.0))
                grown = jnp.exp(col)
                v = conv[:, 2 * DK + r * DV : 2 * DK + (r + 1) * DV]
                right = jnp.concatenate([khat * (beta * grown), v * beta], 1).astype(BF)
                lhs[c, r, :, :DK] = (q * grown).astype(BF)
                lhs[c, r, :, DK:] = jnp.where(incl, qk * decay, 0.0).astype(BF)
                tails[c, r] = (turned * jnp.exp(row[:, CHUNK - 1 :] - row)).astype(BF)
                items.append((c, r, right))
        for (c, r, right), inverse in zip(items, unit_inverse(lowers, row_id, col_id)):
            wu[c, r] = dot(inverse.astype(BF), right).astype(BF)

    def advance(g):
        eye = (iota(0) == iota(1)).astype(F32)
        for r in range(group):
            run[r, :, :DK] = eye
            run[r, :, DK:] = jnp.zeros((DK, DV), F32)

        def body(c, carry):
            states = [run[r] for r in range(group)]
            parts = [s.astype(BF) for s in states]
            news = []
            for r in range(group):
                rhs[c, r, :DK, :] = parts[r]
                got = wu[c, r]
                taken = dot(got[:, :DK], parts[r])
                y = jnp.concatenate([-taken[:, :DK], got[:, DK:].astype(F32) - taken[:, DK:]], 1)
                news.append(y.astype(BF))
            for r in range(group):
                rhs[c, r, DK:, :] = news[r]
                last = jnp.exp(gates[g, c, r : r + 1, CHUNK - 1 :])
                run[r] = last * states[r] + dot(tails[c, r], news[r])
            return carry

        lax.fori_loop(0, chunks, body, 0)
        for r in range(group):
            maps[g, ctx, r * DK : (r + 1) * DK, :] = run[r].astype(BF)

    def outputs(g):
        def body(c, carry):
            place = pl.ds(pl.multiple_of(c * CHUNK, CHUNK), CHUNK)
            for r in range(group):
                got = dot(lhs[c, r], rhs[c, r])
                query[g, place, r * DK : (r + 1) * DK] = got[:, :DK].astype(BF)
                core[g, place, r * DV : (r + 1) * DV] = got[:, DK:]
            return carry

        lax.fori_loop(0, chunks, body, 0)

    def close(g):
        def hop(p, states):
            news = []
            for r in range(group):
                high = states[r].astype(BF)
                low = (states[r] - high.astype(F32)).astype(BF)
                both = maps[g, p, r * DK : (r + 1) * DK, :]
                trans = both[:, :DK]
                news.append(dot(trans, high) + dot(trans, low) + both[:, DK:].astype(F32))
            return tuple(news)

        states = lax.fori_loop(0, ctx, hop, tuple(jnp.zeros((DK, DV), F32) for _ in range(group)))
        states = [s.astype(BF) for s in states]
        gain = gain_ref[...]

        def body(d, carry):
            place = pl.ds(pl.multiple_of(d * rows, rows), rows)
            gate_rows = pl.ds(pl.multiple_of(RIM + d * rows, 16), rows)
            for r in range(group):
                h = g * group + r
                full = core[g, place, r * DV : (r + 1) * DV] + dot(query[g, place, r * DK : (r + 1) * DK], states[r])
                mean = jnp.mean(full * full, -1, keepdims=True)
                value = full * lax.rsqrt(mean + 1e-06) * gain * zed[gate_rows, h * DV : (h + 1) * DV]
                norm[g, d, :, r * DV : (r + 1) * DV] = value.astype(BF)
            return carry

        lax.fori_loop(0, heads, body, 0)

    def share(g):
        copies = [
            pltpu.make_async_remote_copy(
                src_ref=norm.at[g, peer],
                dst_ref=norm_all.at[g, head],
                send_sem=norm_send.at[g, i],
                recv_sem=norm_recv.at[g, i],
                device_id=(ctx, peer),
                device_id_type=MESH,
            )
            for i, peer in enumerate((two, three, one))
        ]
        for copy in copies:
            copy.start()
        keep = pltpu.make_async_copy(norm.at[g, head], norm_all.at[g, head], local_sem.at[g])
        keep.start()
        return copies, keep

    shared = []
    for g in range(key_heads):
        project(g, store_raw)

        def body(i, carry):
            within(g, [2 * i, 2 * i + 1])
            return carry

        lax.fori_loop(0, chunks // 2, body, 0)
        advance(g)
        map_streams[g].start()
        outputs(g)
        relay_all(map_streams[g])
    project(key_heads, store_zed)
    mix_across.wait_recv()
    mix_onward.start()
    for g in range(key_heads):
        map_streams[g].finish()
        close(g)
        shared.append(share(g))
    mix_beside.wait_recv()
    mix_onward.wait_recv()
    for copies, keep in shared:
        for copy in copies:
            copy.wait_recv()
        keep.wait()

    width = group * DV
    out_tile = mix.shape[3] if wide else 256

    def last(p, carry):
        total = jnp.zeros((rows, out_tile), F32)
        for h in range(heads):
            for g in range(key_heads):
                left = norm_all[g, h]
                if wide:
                    total = total + dot(left, mix[h, p, g * width : (g + 1) * width, :])
                else:
                    right = mix[h, pl.ds(pl.multiple_of(p * out_tile, out_tile), out_tile), g * width : (g + 1) * width]
                    total = total + dot(left, right, NT)
        out_ref[:, pl.ds(pl.multiple_of(p * out_tile, out_tile), out_tile)] = total.astype(BF)
        return carry

    lax.fori_loop(0, out_ref.shape[1] // out_tile, last, 0)

    for copy in across + beside + onward + [mix_across, mix_beside, mix_onward]:
        copy.wait_send()

    @pl.when(gives_rim)
    def _():
        for copy in rims:
            copy.wait_send()

    for stream in streams + [mixes] + map_streams:
        stream.drain()
    for copies, keep in shared:
        for copy in copies:
            copy.wait_send()


def shards(activations, w_query, w_key, w_value, w_zgate, conv_query, conv_key, conv_value, gate_code, beta_code, norm_gain, w_out):
    n, heads = lax.axis_size("ctx"), lax.axis_size("head")
    rows, width = activations.shape
    length = rows * heads
    values = gate_code.shape[1]
    key_heads = w_query.shape[1] // DK
    group = values // key_heads
    span = 2 * DK + group * DV
    depth = w_query.shape[0]
    wide = w_out.shape[1] % 256 == 0
    wo = w_out if wide else w_out.T
    mix_shape = (heads, n) + w_out.shape if wide else (heads, n * w_out.shape[1], w_out.shape[0])
    chunks = length // CHUNK
    any_ref = pl.BlockSpec(memory_space=pl.ANY)
    vmem = pl.BlockSpec(memory_space=pltpu.VMEM)
    units = 4 * (n // 2)
    dma = pltpu.SemaphoreType.DMA
    return pl.pallas_call(
        functools.partial(layer_kernel, n, heads, key_heads, group, wide),
        in_specs=[any_ref] * 6 + [vmem] * 6,
        out_specs=vmem,
        out_shape=jax.ShapeDtypeStruct((rows, n * w_out.shape[1]), BF),
        scratch_shapes=[
            pltpu.VMEM((RIM + length, width), BF),
            pltpu.VMEM((key_heads + 1, n * depth, span), BF),
            pltpu.VMEM(mix_shape, BF),
            pltpu.VMEM((RIM + length, span), F32),
            pltpu.VMEM((RIM + length, values * DV), F32),
            pltpu.VMEM((key_heads, chunks, 8, CHUNK), F32),
            pltpu.VMEM((chunks, group, CHUNK, DK + DV), BF),
            pltpu.VMEM((chunks, group, CHUNK, DK + CHUNK), BF),
            pltpu.VMEM((chunks, group, DK + CHUNK, DK + DV), BF),
            pltpu.VMEM((chunks, group, DK, CHUNK), BF),
            pltpu.VMEM((group, DK, DK + DV), F32),
            pltpu.VMEM((key_heads, length, group * DV), F32),
            pltpu.VMEM((key_heads, length, group * DK), BF),
            pltpu.VMEM((key_heads, n, group * DK, DK + DV), BF),
            pltpu.VMEM((key_heads, heads, rows, group * DV), BF),
            pltpu.VMEM((key_heads, heads, rows, group * DV), BF),
            dma((3 * key_heads + 2 + PAIR,)),
            dma((3 * PAIR,)),
            dma((3 * PAIR,)),
            dma((heads,)),
            dma,
            dma((key_heads + 2, units)),
            dma((key_heads + 2, units)),
            dma((key_heads, units)),
            dma((key_heads, units)),
            dma((3,)),
            dma((3,)),
            dma((key_heads, heads - 1)),
            dma((key_heads, heads - 1)),
        ],
        compiler_params=pltpu.CompilerParams(collective_id=0, has_side_effects=True, vmem_limit_bytes=63 * 1024 * 1024),
        name="layer",
    )(
        activations, w_query, w_key, w_value, w_zgate, wo, conv_query, conv_key, conv_value,
        gate_code.T, beta_code.T, norm_gain.reshape(1, DV),
    )


def solution(mesh):
    return jax.shard_map(
        shards,
        mesh=mesh,
        in_specs=(
            P(("ctx", "head"), None),
            P("ctx", "head"),
            P("ctx", "head"),
            P("ctx", "head"),
            P("ctx", "head"),
            P(None, "head"),
            P(None, "head"),
            P(None, "head"),
            P("ctx", "head"),
            P("ctx", "head"),
            P(),
            P("head", "ctx"),
        ),
        out_specs=P(("ctx", "head"), None),
        check_vma=False,
    )
```

time: 333 us -> 170 us (0.51)
  waiting for transfers between devices: 136 us -> 0 us
  matrix products: 20.9 us -> 0 us
  between operations: 13.2 us -> 0.01 us
  Pallas kernels: 154 us -> 167 us
  other arithmetic: 3.64 us -> 0 us
  starting transfers between devices: 3.5 us -> 0 us
    all_gather x2 -> x0, waiting for transfers between devices: 92.6 us -> none  [the longest x1 47.7 us: shards(): maps = lax.all_gather(state, 'ctx', axis=0)]
    reduce_scatter x1 -> x0, waiting for transfers between devices: 42.9 us -> none  [shards(): return lax.psum_scatter(mixed, 'head', scatter_dimension=0, tiled=True)]
    dot_general x3 -> x0, matrix products: 20.9 us -> none  [the longest x2 14.7 us: shards(): jnp.dot(x, w, preferred_element_type=jnp.float32).astype(jnp.bfloat16)]
    pallas_call x3 -> x1, Pallas kernels: 154 us -> 167 us  [shards(): pl.pallas_call(functools.partial(layer_kernel, n, heads, key_heads, group...]
    concatenate x3 -> x0, other arithmetic: 3.63 us -> none  [the longest x1 2.03 us: shards(): jnp.concatenate([w_query, w_key, w_value, w_zgate], 1)]
    ppermute x1 -> x0, starting transfers between devices: 3.41 us -> none  [shards(): lax.ppermute(gathered[length - EDGE:], 'ctx', [(i, i + 1) for i in range(...]
  transfers between devices with their start and end apart: 4 -> 0, of which waited for: 3 -> 0; matrix products, arithmetic and copies ran while one was open for 4% -> 0% of each run, Pallas kernels for 2% -> 0%
where the time goes in v1:
time: 170 us; the launch traced here: 169 us
  Pallas kernels  167 us (98%)
  local copies, waits for them, and re-layouts  2.3 us (1%)
    pallas_call x1, Pallas kernels, shards(): pl.pallas_call(functools.partial(layer_kernel, n, heads, key_heads, group...  167 us

profile of v1, /device:TPU:0, one launch (start us, length us, event | category | flops | bytes accessed | tf_op | source)
XLA Modules:
  0.0 169.2 jit_solution(6615445679964500052)
XLA Ops:
  0.0 166.9 %layer.1 = bf16[256,2048]{1,0:T(8,128)(2,1)} custom-call(bf16[256,2048]{1,0:T(8,128)(2,1)} %act_ref.1, bf16[256,256]{1,0:T(8,128)(2,1)} %wq_ref.1, bf16[256,256]{1,0:T(8,128)(2,1)} %wk_ref.1, bf16[256,512]{1,0:T(8,128)(2,1)} %wv_ref.1, bf16[256,512]{1,0:T(8,128)(2,1)} %wz_ref.1, bf16[512,256]{1,0:T(8,128)(2,1)} %wo_ref.1, bf16[4,256]{1,0:T(4,128)(2,1)} %cq_ref.1, ...), custom_call_target="tpu_custom_call" | custom-call | tf_op jit(solution)/shard_map/layer/pallas_call | solution.py:490
  166.9 2.3 %copy.14 = bf16[256,2048]{1,0:T(8,128)(2,1)} copy(bf16[256,2048]{1,0:T(8,128)(2,1)} %layer.1) | data formatting | bytes 2097152

commit v2 on v1

--- a/solution.py
+++ b/solution.py
@@ -58,7 +58,7 @@
                         device_id=(after if way == 0 else before, head),
                         device_id_type=MESH,
                     )
-        self.owner = lambda s, way: ring_device(lax.rem(position + (n - s if way == 0 else s), n), n)
+        self.arrived = lambda s, way: ring_device(lax.rem(position + (n - s - 1 if way == 0 else s + 1), n), n)
         self.waited = set()
 
     def start(self):
@@ -75,10 +75,21 @@
                     self.waited.add((s - 1, way, half))
                     self.units[s, way, half].start()
 
+    def bundle(self, k, parts=3, then=lambda s: None):
+        for s in range(1, self.reach):
+            if (s - 1) * parts // max(self.reach - 1, 1) == k:
+                self.relay(s)
+                then(s - 1)
+
+    def settle(self, s):
+        for key, unit in self.units.items():
+            if key[0] == s and key not in self.waited:
+                unit.wait_recv()
+                self.waited.add(key)
+
     def finish(self):
-        for key, unit in self.units.items():
-            if key not in self.waited:
-                unit.wait_recv()
+        for s in range(self.reach):
+            self.settle(s)
 
     def drain(self):
         for unit in self.units.values():
@@ -110,8 +121,8 @@
     n, heads, key_heads, group, wide,
     act_ref, wq_ref, wk_ref, wv_ref, wz_ref, wo_ref, cq_ref, ck_ref, cv_ref, gate_ref, beta_ref, gain_ref,
     out_ref,
-    act, weight, mix, raw, zed, gates, wu, lhs, rhs, tails, run, core, query, maps, norm, norm_all,
-    local_sem, act_send, act_recv, rim_send, rim_recv, ring_send, ring_recv, map_send, map_recv, mix_send, mix_recv, norm_send, norm_recv,
+    act, weight, zweight, mix, raw, zed, gates, wu, lhs, rhs, tails, run, core, query, enter, leave, norm, norm_all,
+    local_sem, act_send, act_recv, rim_send, rim_recv, ring_send, ring_recv, pass_send, pass_recv, mix_send, mix_recv, norm_send, norm_recv,
 ):
     ctx, head = lax.axis_index("ctx"), lax.axis_index("head")
     one = head + 1 - 2 * lax.rem(head, 2)
@@ -123,9 +134,9 @@
     chunks = length // CHUNK
     span = 2 * DK + group * DV
 
-    def weight_view(g):
+    def weight_view(buffer, g):
         def view(owner, half):
-            return weight.at[g, pl.ds(pl.multiple_of(owner * depth + half * (depth // 2), depth // 2), depth // 2)]
+            return buffer.at[g, pl.ds(pl.multiple_of(owner * depth + half * (depth // 2), depth // 2), depth // 2)]
 
         return view
 
@@ -143,7 +154,8 @@
         mine.append((wq_ref.at[:, pl.ds(g * DK, DK)], weight.at[g, place, pl.ds(0, DK)]))
         mine.append((wk_ref.at[:, pl.ds(g * DK, DK)], weight.at[g, place, pl.ds(DK, DK)]))
         mine.append((wv_ref.at[:, pl.ds(g * group * DV, group * DV)], weight.at[g, place, pl.ds(2 * DK, group * DV)]))
-    mine.append((wz_ref, weight.at[key_heads, place]))
+    for g in range(key_heads):
+        mine.append((wz_ref.at[:, pl.ds(g * group * DV, group * DV)], zweight.at[g, place]))
     mine.append((wo_ref, mix_slot(head, ctx)))
     block = lambda h, sub: act.at[pl.ds(pl.multiple_of(RIM + h * rows + sub * (rows // PAIR), 16), rows // PAIR)]
     piece = lambda sub: act_ref.at[pl.ds(sub * (rows // PAIR), rows // PAIR)]
@@ -167,7 +179,16 @@
     def _():
         pl.semaphore_signal(barrier, inc=1, device_id=(ctx - 1, heads - 1), device_id_type=MESH)
 
-    pl.semaphore_wait(barrier, 5 + heads * gives_rim.astype(jnp.int32))
+    @pl.when(ctx > 0)
+    def _():
+        pl.semaphore_signal(barrier, inc=1, device_id=(ctx - 1, head), device_id_type=MESH)
+
+    @pl.when(ctx < n - 1)
+    def _():
+        pl.semaphore_signal(barrier, inc=1, device_id=(ctx + 1, head), device_id_type=MESH)
+
+    inner = (ctx > 0).astype(jnp.int32) + (ctx < n - 1).astype(jnp.int32)
+    pl.semaphore_wait(barrier, 5 + inner + heads * gives_rim.astype(jnp.int32))
 
     def to_peer(src, dst, index, peer):
         return pltpu.make_async_remote_copy(
@@ -188,12 +209,10 @@
         )
         for h in range(heads)
     ]
-    streams = [Stream(n, weight_view(g), ring_send.at[g], ring_recv.at[g]) for g in range(key_heads + 1)]
-    mixes = Stream(n, lambda owner, half: mix_slot(head, owner, half), ring_send.at[key_heads + 1], ring_recv.at[key_heads + 1])
-    map_streams = [
-        Stream(n, lambda owner, half, g=g: maps.at[g, owner, pl.ds(half * group * DK // 2, group * DK // 2)], map_send.at[g], map_recv.at[g])
-        for g in range(key_heads)
-    ]
+    stream = lambda view, i: Stream(n, view, ring_send.at[i], ring_recv.at[i])
+    streams = [stream(weight_view(weight, g), g) for g in range(key_heads)]
+    zeds = [stream(weight_view(zweight, g), key_heads + g) for g in range(key_heads)]
+    mixes = stream(lambda owner, half: mix_slot(head, owner, half), 2 * key_heads)
 
     @pl.when(gives_rim)
     def _():
@@ -232,47 +251,62 @@
                 gates[g, c, group + r : group + r + 1, :] = betas[h : h + 1, c * CHUNK : (c + 1) * CHUNK]
             gates[g, c, 2 * group :, :] = jnp.zeros((8 - 2 * group, CHUNK), F32)
 
-    def relay_all(stream):
-        for s in range(1, stream.reach):
-            stream.relay(s)
-
-    for s in range(1, streams[0].reach):
-        streams[0].relay(s)
-    for stream in streams[1:]:
-        stream.start()
-        relay_all(stream)
-    mixes.start()
-    relay_all(mixes)
-    for a, b in zip(across, onward):
-        a.wait_recv()
-        b.start()
-
-    @pl.when(ctx > 0)
-    def _():
-        rims[0].wait_recv()
-
-    for copy in beside + onward:
-        copy.wait_recv()
-    for stream in streams + [mixes]:
-        stream.finish()
-
-    def mix_copy(src, index, peer):
+    def mix_copy(h, owner, half, kind, index, peer):
+        place = mix_slot(h, owner, half)
         return pltpu.make_async_remote_copy(
-            src_ref=src, dst_ref=src, send_sem=mix_send.at[index], recv_sem=mix_recv.at[index], device_id=(ctx, peer), device_id_type=MESH
+            src_ref=place, dst_ref=place, send_sem=mix_send.at[kind, index], recv_sem=mix_recv.at[kind, index], device_id=(ctx, peer), device_id_type=MESH
         )
 
-    mix_across = mix_copy(mix.at[head], 0, two)
-    mix_beside = mix_copy(mix.at[head], 1, one)
-    mix_onward = mix_copy(mix.at[two], 2, one)
-    mix_across.start()
-    mix_beside.start()
-
-    def project(g, store):
+    def mix_group(keys):
+        found = []
+        for owner, half, index in keys:
+            found.append(
+                (
+                    mix_copy(head, owner, half, 0, index, two),
+                    mix_copy(head, owner, half, 1, index, one),
+                    mix_copy(two, owner, half, 2, index, one),
+                )
+            )
+        return found
+
+    mix_sets = [mix_group([(ctx, half, half) for half in range(2)])]
+    for s in range(mixes.reach):
+        keys = [(mixes.arrived(s, way), half, 2 + (s * 2 + way) * 2 + half) for half in range(2) for way in range(2) if (s, way, half) in mixes.units]
+        mix_sets.append(mix_group(keys))
+
+    def mix_forward(s):
+        for across_copy, beside_copy, _ in mix_sets[s]:
+            across_copy.start()
+            beside_copy.start()
+
+    def mix_onward(s):
+        for across_copy, _, onward_copy in mix_sets[s]:
+            across_copy.wait_recv()
+            onward_copy.start()
+
+    onward_done = [0]
+
+    def mix_catch_up(share, shares):
+        stop = (mixes.reach + 1) * share // shares
+        while onward_done[0] < stop:
+            mix_onward(onward_done[0])
+            onward_done[0] += 1
+
+    def hooked(count, body, hooks):
+        def step(i, carry):
+            for j, hook in hooks.items():
+                pl.when(i == j)(hook)
+            body(i)
+            return carry
+
+        lax.fori_loop(0, count, step, 0)
+
+    def project(matrix, store):
         tile = (length + RIM) // 5
 
         def body(m, carry):
             start = pl.multiple_of(m * tile, 16)
-            store(start, tile, dot(act[pl.ds(start, tile), :], weight[g]))
+            store(start, tile, dot(act[pl.ds(start, tile), :], matrix[...]))
             return carry
 
         lax.fori_loop(0, 5, body, 0)
@@ -280,8 +314,11 @@
     def store_raw(start, tile, value):
         raw[pl.ds(start, tile), :] = value
 
-    def store_zed(start, tile, value):
-        zed[pl.ds(start, tile), :] = silu(value)
+    def store_zed(g):
+        def store(start, tile, value):
+            zed[g, pl.ds(start, tile), :] = silu(value)
+
+        return store
 
     def within(g, chunk_list):
         row_id, col_id = iota(0), iota(1)
@@ -330,11 +367,11 @@
     def advance(g):
         eye = (iota(0) == iota(1)).astype(F32)
         for r in range(group):
-            run[r, :, :DK] = eye
-            run[r, :, DK:] = jnp.zeros((DK, DV), F32)
+            run[g, r, :, :DK] = eye
+            run[g, r, :, DK:] = jnp.zeros((DK, DV), F32)
 
         def body(c, carry):
-            states = [run[r] for r in range(group)]
+            states = [run[g, r] for r in range(group)]
             parts = [s.astype(BF) for s in states]
             news = []
             for r in range(group):
@@ -346,12 +383,40 @@
             for r in range(group):
                 rhs[c, r, DK:, :] = news[r]
                 last = jnp.exp(gates[g, c, r : r + 1, CHUNK - 1 :])
-                run[r] = last * states[r] + dot(tails[c, r], news[r])
+                run[g, r] = last * states[r] + dot(tails[c, r], news[r])
             return carry
 
         lax.fori_loop(0, chunks, body, 0)
-        for r in range(group):
-            maps[g, ctx, r * DK : (r + 1) * DK, :] = run[r].astype(BF)
+
+    passes = [
+        pltpu.make_async_remote_copy(
+            src_ref=leave.at[g],
+            dst_ref=enter.at[g],
+            send_sem=pass_send.at[g],
+            recv_sem=pass_recv.at[g],
+            device_id=(lax.rem(ctx + 1, n), head),
+            device_id_type=MESH,
+        )
+        for g in range(key_heads)
+    ]
+
+    def chain(g, point, points=8):
+        @pl.when(lax.div(ctx * points, n) == point)
+        def _():
+            @pl.when(ctx == 0)
+            def _():
+                enter[g] = jnp.zeros(enter.shape[1:], BF)
+
+            @pl.when(ctx > 0)
+            def _():
+                passes[g].wait_recv()
+
+            @pl.when(ctx < n - 1)
+            def _():
+                for r in range(group):
+                    both = run[g, r]
+                    leave[g, r] = (dot(both[:, :DK].astype(BF), enter[g, r]) + both[:, DK:]).astype(BF)
+                passes[g].start()
 
     def outputs(g):
         def body(c, carry):
@@ -365,28 +430,16 @@
         lax.fori_loop(0, chunks, body, 0)
 
     def close(g):
-        def hop(p, states):
-            news = []
-            for r in range(group):
-                high = states[r].astype(BF)
-                low = (states[r] - high.astype(F32)).astype(BF)
-                both = maps[g, p, r * DK : (r + 1) * DK, :]
-                trans = both[:, :DK]
-                news.append(dot(trans, high) + dot(trans, low) + both[:, DK:].astype(F32))
-            return tuple(news)
-
-        states = lax.fori_loop(0, ctx, hop, tuple(jnp.zeros((DK, DV), F32) for _ in range(group)))
-        states = [s.astype(BF) for s in states]
+        states = [enter[g, r] for r in range(group)]
         gain = gain_ref[...]
 
         def body(d, carry):
             place = pl.ds(pl.multiple_of(d * rows, rows), rows)
             gate_rows = pl.ds(pl.multiple_of(RIM + d * rows, 16), rows)
             for r in range(group):
-                h = g * group + r
                 full = core[g, place, r * DV : (r + 1) * DV] + dot(query[g, place, r * DK : (r + 1) * DK], states[r])
                 mean = jnp.mean(full * full, -1, keepdims=True)
-                value = full * lax.rsqrt(mean + 1e-06) * gain * zed[gate_rows, h * DV : (h + 1) * DV]
+                value = full * lax.rsqrt(mean + 1e-06) * gain * zed[g, gate_rows, r * DV : (r + 1) * DV]
                 norm[g, d, :, r * DV : (r + 1) * DV] = value.astype(BF)
             return carry
 
@@ -410,28 +463,106 @@
         keep.start()
         return copies, keep
 
+    first, later = streams[0], streams[1:]
+    queue = later + [mixes] + zeds
+    def pass_mix(s):
+        mixes.settle(s)
+        mix_forward(s + 1)
+
+    notes = {id(mixes): pass_mix}
+    steps = []
+    for i, one_stream in enumerate([first] + queue):
+        for k in range(3):
+            steps.append((one_stream, k, queue[i] if k == 2 and i < len(queue) else None))
+    steps.reverse()
+
+    def step():
+        if steps:
+            one_stream, k, following = steps.pop()
+            one_stream.bundle(k, 3, notes.get(id(one_stream), lambda s: None))
+            if following is not None:
+                following.start()
+
+    step()
+    step()
+    across[0].wait_recv()
+    onward[0].start()
+    step()
+    across[1].wait_recv()
+    onward[1].start()
+    mix_forward(0)
+
+    @pl.when(ctx > 0)
+    def _():
+        rims[0].wait_recv()
+
+    for copy in beside + onward:
+        copy.wait_recv()
+    first.finish()
+
     shared = []
     for g in range(key_heads):
-        project(g, store_raw)
-
-        def body(i, carry):
+        if g > 0:
+            streams[g].finish()
+        project(weight.at[g], store_raw)
+        step()
+        if g > 0:
+            chain(g - 1, 1)
+
+        def body(i):
             within(g, [2 * i, 2 * i + 1])
-            return carry
-
-        lax.fori_loop(0, chunks // 2, body, 0)
+
+        def hook(k):
+            def run_hook():
+                if g > 0:
+                    chain(g - 1, 2 + k)
+                if k % 2 == 1:
+                    step()
+
+            return run_hook
+
+        hooked(chunks // 2, body, {k: hook(k) for k in range(4)})
         advance(g)
-        map_streams[g].start()
+        if g > 0:
+            chain(g - 1, 6)
+        chain(g, 0)
         outputs(g)
-        relay_all(map_streams[g])
-    project(key_heads, store_zed)
-    mix_across.wait_recv()
-    mix_onward.start()
+        if g > 0:
+            chain(g - 1, 7)
+    last_group = key_heads - 1
+    mixes.finish()
+    mix_forward(mixes.reach)
+    mix_catch_up(1, 4)
+    step()
+    chain(last_group, 1)
+    step()
+    chain(last_group, 2)
+    step()
+    mix_catch_up(2, 4)
+    chain(last_group, 3)
     for g in range(key_heads):
-        map_streams[g].finish()
-        close(g)
-        shared.append(share(g))
-    mix_beside.wait_recv()
-    mix_onward.wait_recv()
+        zeds[g].finish()
+        project(zweight.at[g], store_zed(g))
+        if g < last_group:
+            step()
+            chain(last_group, 4)
+            close(g)
+            shared.append(share(g))
+            step()
+            chain(last_group, 5)
+            mix_catch_up(3, 4)
+            step()
+            chain(last_group, 6)
+    chain(last_group, 7)
+    close(last_group)
+    shared.append(share(last_group))
+    while steps:
+        step()
+    mix_catch_up(4, 4)
+    for group_copies in mix_sets:
+        for _, beside_copy, onward_copy in group_copies:
+            beside_copy.wait_recv()
+            onward_copy.wait_recv()
     for copies, keep in shared:
         for copy in copies:
             copy.wait_recv()
@@ -455,16 +586,25 @@
 
     lax.fori_loop(0, out_ref.shape[1] // out_tile, last, 0)
 
-    for copy in across + beside + onward + [mix_across, mix_beside, mix_onward]:
+    for copy in across + beside + onward:
         copy.wait_send()
+    for group_copies in mix_sets:
+        for copies in group_copies:
+            for copy in copies:
+                copy.wait_send()
+
+    @pl.when(ctx < n - 1)
+    def _():
+        for copy in passes:
+            copy.wait_send()
 
     @pl.when(gives_rim)
     def _():
         for copy in rims:
             copy.wait_send()
 
-    for stream in streams + [mixes] + map_streams:
-        stream.drain()
+    for one_stream in [first] + queue:
+        one_stream.drain()
     for copies, keep in shared:
         for copy in copies:
             copy.wait_send()
@@ -494,32 +634,34 @@
         out_shape=jax.ShapeDtypeStruct((rows, n * w_out.shape[1]), BF),
         scratch_shapes=[
             pltpu.VMEM((RIM + length, width), BF),
-            pltpu.VMEM((key_heads + 1, n * depth, span), BF),
+            pltpu.VMEM((key_heads, n * depth, span), BF),
+            pltpu.VMEM((key_heads, n * depth, group * DV), BF),
             pltpu.VMEM(mix_shape, BF),
             pltpu.VMEM((RIM + length, span), F32),
-            pltpu.VMEM((RIM + length, values * DV), F32),
+            pltpu.VMEM((key_heads, RIM + length, group * DV), F32),
             pltpu.VMEM((key_heads, chunks, 8, CHUNK), F32),
             pltpu.VMEM((chunks, group, CHUNK, DK + DV), BF),
             pltpu.VMEM((chunks, group, CHUNK, DK + CHUNK), BF),
             pltpu.VMEM((chunks, group, DK + CHUNK, DK + DV), BF),
             pltpu.VMEM((chunks, group, DK, CHUNK), BF),
-            pltpu.VMEM((group, DK, DK + DV), F32),
+            pltpu.VMEM((key_heads, group, DK, DK + DV), F32),
             pltpu.VMEM((key_heads, length, group * DV), F32),
             pltpu.VMEM((key_heads, length, group * DK), BF),
-            pltpu.VMEM((key_heads, n, group * DK, DK + DV), BF),
+            pltpu.VMEM((key_heads, group, DK, DV), BF),
+            pltpu.VMEM((key_heads, group, DK, DV), BF),
             pltpu.VMEM((key_heads, heads, rows, group * DV), BF),
             pltpu.VMEM((key_heads, heads, rows, group * DV), BF),
-            dma((3 * key_heads + 2 + PAIR,)),
+            dma((4 * key_heads + 1 + PAIR,)),
             dma((3 * PAIR,)),
             dma((3 * PAIR,)),
             dma((heads,)),
             dma,
-            dma((key_heads + 2, units)),
-            dma((key_heads + 2, units)),
-            dma((key_heads, units)),
-            dma((key_heads, units)),
-            dma((3,)),
-            dma((3,)),
+            dma((2 * key_heads + 1, units)),
+            dma((2 * key_heads + 1, units)),
+            dma((key_heads,)),
+            dma((key_heads,)),
+            dma((3, units + 2)),
+            dma((3, units + 2)),
             dma((key_heads, heads - 1)),
             dma((key_heads, heads - 1)),
         ],

time: 170 us -> 130 us (0.76)
  Pallas kernels: 167 us -> 125 us
    pallas_call x1, Pallas kernels: 167 us -> 125 us  [shards(): pl.pallas_call(functools.partial(layer_kernel, n, heads, key_heads, group...]
where the time goes in v2:
time: 130 us; the launch traced here: 128 us
  Pallas kernels  125 us (96%)
  local copies, waits for them, and re-layouts  2.3 us (2%)
    pallas_call x1, Pallas kernels, shards(): pl.pallas_call(functools.partial(layer_kernel, n, heads, key_heads, group...  125 us

profile of v2, /device:TPU:0, one launch (start us, length us, event | category | flops | bytes accessed | tf_op | source)
XLA Modules:
  0.0 127.7 jit_solution(8003313852209775713)
XLA Ops:
  0.0 125.4 %layer.1 = bf16[256,2048]{1,0:T(8,128)(2,1)} custom-call(bf16[256,2048]{1,0:T(8,128)(2,1)} %act_ref.1, bf16[256,256]{1,0:T(8,128)(2,1)} %wq_ref.1, bf16[256,256]{1,0:T(8,128)(2,1)} %wk_ref.1, bf16[256,512]{1,0:T(8,128)(2,1)} %wv_ref.1, bf16[256,512]{1,0:T(8,128)(2,1)} %wz_ref.1, bf16[512,256]{1,0:T(8,128)(2,1)} %wo_ref.1, bf16[4,256]{1,0:T(4,128)(2,1)} %cq_ref.1, ...), custom_call_target="tpu_custom_call" | custom-call | tf_op jit(solution)/shard_map/layer/pallas_call | solution.py:630
  125.4 2.3 %copy.14 = bf16[256,2048]{1,0:T(8,128)(2,1)} copy(bf16[256,2048]{1,0:T(8,128)(2,1)} %layer.1) | data formatting | bytes 2097152
